TPU v7x, 32 devices: a whole 2x2x4 slice. The times are simulated.
32 devices in a mesh: grp: 2 (over y), ta: 4 (over z), gx: 4 (over x, core).
Axes of the slice: x: 2, y: 2, z: 4, core: 2. Of those that a mesh axis runs over, the one named last changes fastest.
Arguments:
- vectors: bfloat16 [8, 2, 3, 8192, 128], P(('grp', 'ta'), None, None, 'gx'), parts along dimension 0, may hold values from -6 to 6
- peramb: bfloat16 [8, 16, 2, 128, 128], P(('grp', 'ta')), parts along dimension 0, may hold values from -0.5 to 0.5
- momenta: int32 [8, 3], P('grp'), parts along dimension 0, may hold values from -2 to 2, as said below
- sink_mom: int32 [32], P('grp'), parts along dimension 0, may hold values from 0 to 3
- spin_pick: int32 [32], P('grp'), parts along dimension 0, may hold values from 0 to 15
- src_time: int32 [2], P('grp'), parts along dimension 0, may hold values from 0 to 65535
Outputs:
- corr: float32 [8, 16, 2, 128, 128], P(('grp', 'ta'), 'gx'), parts along dimension 0
There are 2 independent parts, one for each index of `grp`. A program takes and returns all parts, laid end to end along the dimension named above; each array names one. Nothing has to cross between parts.
Inputs may be any that keep to these rules, and one draw needn't show every extreme that they name: `momenta`: every component of every momentum is nonzero.
All inputs are finite; a program needn't handle non-finite values.
Results may differ from a plain program's by a relative error of at most 0.0038.
Values sent between devices are 32-bit elements; how exact they have to be, the bound alone decides.
A program may use at most 64 MiB of HBM per device.

v0:
```python
import functools
import math

import jax
import jax.numpy as jnp
from jax import lax
from jax.experimental import pallas as pl
from jax.experimental.pallas import tpu as pltpu
from jax.sharding import PartitionSpec as P

LY = 32
LZ = 32
MESH = pl.DeviceIdType.MESH
F32 = jnp.float32
BF16 = jnp.bfloat16


def split(value):
    high = value.astype(BF16)
    low = (value - high.astype(F32)).astype(BF16)
    return high, low


def mxu(left, right):
    return lax.dot_general(left, right, (((1,), (0,)), ((), ())), preferred_element_type=F32)


def complex_block(re, im):
    return jnp.concatenate(
        [jnp.concatenate([re, im], axis=1), jnp.concatenate([-im, re], axis=1)], axis=0
    )


def kernel(
    n, nt, chunk, piece,
    mom_hbm, sink_hbm, pick_hbm, time_hbm, vec_hbm, per_hbm,
    out_ref,
    mom_ref, sink_ref, pick_ref, time_ref,
    ab, trans, trig, acc, per, part, rx1, s1, rx2, full, tabuf, src, half,
    outbuf, out_sem, int_sem, vec_sem, per_sem, ta_s, ta_r, sl_s, sl_r,
    x1_s, x1_r, x2_s, x2_r, x3_s, x3_r,
):
    nmom = part.shape[0]
    rank = part.shape[-1]
    colours, sites = ab.shape[0], ab.shape[1]
    blocks = out_ref.shape[1]
    rows = rank // n
    hrows = rank // 2
    g = lax.axis_index("gx")
    t = lax.axis_index("ta")
    core = lax.rem(g, 2)
    partner = g + 1 - 2 * core
    chips = n // 2

    def ahead(d):
        return lax.rem(g + d, n)

    def remote(src_ref, dst_ref, ss, rs, **where):
        return pltpu.make_async_remote_copy(
            src_ref=src_ref, dst_ref=dst_ref, send_sem=ss, recv_sem=rs,
            device_id=where, device_id_type=MESH,
        )

    integers = [
        pltpu.make_async_copy(where, to, int_sem.at[i])
        for i, (where, to) in enumerate(
            [(mom_hbm, mom_ref), (sink_hbm, sink_ref), (pick_hbm, pick_ref), (time_hbm, time_ref)]
        )
    ]
    for load in integers:
        load.start()
    barrier = pltpu.get_barrier_semaphore()
    for d in range(1, n):
        pl.semaphore_signal(barrier, inc=1, device_id={"gx": ahead(d)}, device_id_type=MESH)
    for d in range(1, nt):
        pl.semaphore_signal(
            barrier, inc=1, device_id={"ta": lax.rem(t + d, nt)}, device_id_type=MESH
        )

    loads = []
    for col in range(colours):
        for ri in range(2):
            load = pltpu.make_async_copy(
                vec_hbm.at[0, ri, col],
                ab.at[col, :, pl.ds(ri * rank, rank)],
                vec_sem.at[col, ri],
            )
            load.start()
            loads.append(load)
    per_load = pltpu.make_async_copy(per_hbm.at[0], per, per_sem)
    per_load.start()

    for load in integers:
        load.wait()

    slab_x = sites // (LY * LZ)
    shape = (8, sites)
    row = lax.broadcasted_iota(jnp.int32, shape, 0)
    site = lax.broadcasted_iota(jnp.int32, shape, 1)

    def component(axis):
        value = jnp.zeros(shape, F32)
        for m in range(nmom):
            value = jnp.where(row == m, mom_ref[m, axis].astype(F32), value)
        return value

    x = (g * slab_x + lax.shift_right_logical(site, int(math.log2(LY * LZ)))).astype(F32)
    y = (lax.shift_right_logical(site, int(math.log2(LZ))) & (LY - 1)).astype(F32)
    z = (site & (LZ - 1)).astype(F32)
    turns = (
        component(0) * x * (1.0 / (slab_x * n))
        + component(1) * y * (1.0 / LY)
        + component(2) * z * (1.0 / LZ)
    )
    turns = turns - jnp.floor(turns + 0.5)
    angle = (2.0 * math.pi) * turns
    trig[0] = jnp.cos(angle)
    trig[1] = jnp.sin(angle)

    scale = 1.0 / math.sqrt(colours * sites * n)

    def accumulate(p, col):
        @pl.loop(0, sites // chunk)
        def _(i):
            at = pl.ds(pl.multiple_of(i * chunk, chunk), chunk)
            a = trans[col, 0, :, at]
            b = trans[col, 1, :, at]
            c = trig[0, p : p + 1, at]
            s = trig[1, p : p + 1, at]
            phased = jnp.concatenate(
                [(a * c + b * s).astype(BF16), (b * c - a * s).astype(BF16)], axis=0
            )
            acc[...] += mxu(phased, ab[col, at, :])

    def finish(p):
        part[p, 0] = (acc[:rank, :rank] + acc[rank:, rank:]).T * scale
        part[p, 1] = (acc[rank:, :rank] - acc[:rank, rank:]).T * scale

    def band(at, size):
        return pl.ds(pl.multiple_of(at * size, size), size)

    mine = pl.ds(pl.multiple_of(core * hrows + lax.div(g, 2) * rows, rows), rows)
    sends = []

    def ta_copy(d):
        return remote(
            tabuf.at[t], tabuf.at[t], ta_s.at[d - 1], ta_r.at[d - 1], ta=lax.rem(t + d, nt)
        )

    def sl_copy(d):
        return remote(
            src.at[:, mine], src.at[:, mine], sl_s.at[d - 1], sl_r.at[d - 1], gx=ahead(d)
        )

    def x1_copy(p):
        return remote(
            part.at[p, :, band(1 - core, hrows)], rx1.at[p], x1_s.at[p], x1_r.at[p],
            gx=partner,
        )

    def x2_copy(p, d):
        return remote(
            s1.at[p], rx2.at[p, d - 1], x2_s.at[p, d - 1], x2_r.at[p, d - 1],
            gx=ahead(2 * d),
        )

    def x3_copy(p):
        keep = full.at[p, :, band(core, hrows)]
        return remote(keep, keep, x3_s.at[p], x3_r.at[p], gx=partner)

    def go(copy):
        copy.start()
        sends.append(copy)

    def p0_select():
        for d in range(1, nt):
            ta_copy(d).wait_recv()
        root = lax.rem(time_ref[0], nt)
        src[:, mine] = tabuf[root]
        for d in range(1, n):
            go(sl_copy(d))

    def step2(p):
        x1_copy(p).wait_recv()
        s1[p] = part[p, :, band(core, hrows)] + rx1[p]
        for d in range(1, chips):
            go(x2_copy(p, d))

    def step3(p):
        total = s1[p]
        for d in range(1, chips):
            x2_copy(p, d).wait_recv()
            total = total + rx2[p, d - 1]
        full[p, :, band(core, hrows)] = total
        if p == 0:
            tabuf[t] = full[0, :, mine]
            for d in range(1, nt):
                go(ta_copy(d))
        go(x3_copy(p))

    acc[...] = jnp.zeros_like(acc)
    for col in range(colours):
        loads[2 * col].wait()
        loads[2 * col + 1].wait()

        @pl.loop(0, sites // piece)
        def _(i):
            at = pl.ds(pl.multiple_of(i * piece, piece), piece)
            for ri in range(2):
                trans[col, ri, :, at] = ab[col, at, ri * rank : (ri + 1) * rank].astype(F32).T

        accumulate(0, col)
    finish(0)
    pl.semaphore_wait(barrier, n + nt - 2)
    go(x1_copy(0))
    for p in range(1, nmom):
        acc[...] = jnp.zeros_like(acc)
        for col in range(colours):
            accumulate(p, col)
        finish(p)
        go(x1_copy(p))
        if p == 1:
            step2(0)
        if p == 3:
            step2(1)
    if nmom == 1:
        step2(0)
    step3(0)
    for p in range(2 if nmom > 3 else 1, nmom):
        step2(p)
    for p in range(1, nmom):
        if p == nmom - 1:
            p0_select()
        step3(p)
    if nmom == 1:
        p0_select()

    per_load.wait()
    for p in range(nmom):
        x3_copy(p).wait_recv()
    for j in range(blocks):
        sink = sink_ref[g * blocks + j]
        pick = pick_ref[g * blocks + j]
        e_high, e_low = split(jnp.concatenate([full[sink, 0], full[sink, 1]], axis=1))
        spin = complex_block(per[pick, 0], per[pick, 1])
        half[j * rank : (j + 1) * rank] = mxu(e_high, spin) + mxu(e_low, spin)
    h_high, h_low = split(half[...] * (1.0 / math.sqrt(rank)))
    for d in range(1, n):
        sl_copy(d).wait_recv()
    s_high, s_low = split(complex_block(src[0], src[1]))
    stores = []
    for j in range(blocks):
        at = slice(j * rank, (j + 1) * rank)
        corr = mxu(h_high[at], s_high) + mxu(h_high[at], s_low) + mxu(h_low[at], s_high)
        outbuf[j, 0] = corr[:, :rank]
        outbuf[j, 1] = corr[:, rank:]
        store = pltpu.make_async_copy(outbuf.at[j], out_ref.at[0, j], out_sem.at[j])
        store.start()
        stores.append(store)
    for store in stores:
        store.wait()
    for copy in sends:
        copy.wait_send()


def body(vectors, peramb, momenta, sink_mom, spin_pick, src_time):
    n = lax.axis_size("gx")
    nt = lax.axis_size("ta")
    colours, sites, rank = vectors.shape[2:]
    nmom = momenta.shape[0]
    spins = sink_mom.shape[0]
    blocks = spins // n
    rows = rank // n
    chips = n // 2
    chunk = min(2048, sites)
    dma = pltpu.SemaphoreType.DMA
    hbm = pl.BlockSpec(memory_space=pl.ANY)
    return pl.pallas_call(
        functools.partial(kernel, n, nt, chunk, min(2048, sites)),
        out_shape=jax.ShapeDtypeStruct((1, blocks, 2, rank, rank), F32),
        in_specs=[hbm] * 6,
        out_specs=hbm,
        scratch_shapes=[
            pltpu.SMEM(momenta.shape, jnp.int32),
            pltpu.SMEM(sink_mom.shape, jnp.int32),
            pltpu.SMEM(spin_pick.shape, jnp.int32),
            pltpu.SMEM(src_time.shape, jnp.int32),
            pltpu.VMEM((colours, sites, 2 * rank), BF16),
            pltpu.VMEM((colours, 2, rank, sites), F32),
            pltpu.VMEM((2, 8, sites), F32),
            pltpu.VMEM((2 * rank, 2 * rank), F32),
            pltpu.VMEM(peramb.shape[1:], BF16),
            pltpu.VMEM((nmom, 2, rank, rank), F32),
            pltpu.VMEM((nmom, 2, rank // 2, rank), F32),
            pltpu.VMEM((nmom, 2, rank // 2, rank), F32),
            pltpu.VMEM((nmom, max(chips - 1, 1), 2, rank // 2, rank), F32),
            pltpu.VMEM((nmom, 2, rank, rank), F32),
            pltpu.VMEM((nt, 2, rows, rank), F32),
            pltpu.VMEM((2, rank, rank), F32),
            pltpu.VMEM((blocks * rank, 2 * rank), F32),
            pltpu.VMEM((blocks, 2, rank, rank), F32),
            dma((blocks,)),
            dma((4,)),
            dma((colours, 2)),
            dma,
            dma((max(nt - 1, 1),)), dma((max(nt - 1, 1),)),
            dma((n - 1,)), dma((n - 1,)),
            dma((nmom,)), dma((nmom,)),
            dma((nmom, max(chips - 1, 1))), dma((nmom, max(chips - 1, 1))),
            dma((nmom,)), dma((nmom,)),
        ],
        compiler_params=pltpu.CompilerParams(
            collective_id=0, has_side_effects=True, vmem_limit_bytes=67043328
        ),
    )(momenta, sink_mom, spin_pick, src_time, vectors, peramb)


def solution(mesh):
    placed = (
        P(("grp", "ta"), None, None, "gx", None),
        P(("grp", "ta"), None, None, None, None),
        P("grp", None),
        P("grp"),
        P("grp"),
        P("grp"),
    )
    return jax.shard_map(
        body,
        mesh=mesh,
        in_specs=placed,
        out_specs=P(("grp", "ta"), "gx", None, None, None),
        check_vma=False,
    )
```

profile of v0, /device:TPU:0, one launch (start us, length us, event | category | flops | bytes accessed | tf_op | source)
XLA Modules:
  0.0 23.5 jit_solution(687971349090359487)
XLA Ops:
  0.7 21.0 %shard_map.64 = f32[1,4,2,128,128]{4,3,2,1,0:T(8,128)} custom-call(s32[4,3]{1,0:T(4,128)} %mom_hbm.1, s32[16]{0:T(128)} %sink_hbm.1, s32[16]{0:T(128)} %pick_hbm.1, s32[1]{0:T(128)S(6)} %copy.8.time_hbm, bf16[1,2,3,2048,128]{4,3,2,1,0:T(8,128)(2,1)} %vec_hbm.1, bf16[1,16,2,128,128]{4,3,2,1,0:T(8,128)(2,1)} %per_hbm.1), custom_call_target="tpu_custom_call" | custom-call | tf_op jit(solution)/shard_map/pallas_call | solution.py:278
  21.7 1.9 %copy.9 = f32[1,4,2,128,128]{4,3,2,1,0:T(8,128)} copy(f32[1,4,2,128,128]{4,3,2,1,0:T(8,128)} %shard_map.64) | data formatting | bytes 1048576
where the time goes:
time: 23.7 us; the launch traced here: 23.5 us
  Pallas kernels  21 us (89%)
  local copies, waits for them, and re-layouts  1.87 us (8%)
  between operations  0.66 us (3%)
    pallas_call x1, Pallas kernels, body(): pl.pallas_call(functools.partial(kernel, n, nt, chunk, min(2048, sites)),...  21 us
    unnamed x1, local copies, waits for them, and re-layouts  1.87 us

commit v1 on v0

--- a/solution.py
+++ b/solution.py
@@ -37,7 +37,7 @@
     out_ref,
     mom_ref, sink_ref, pick_ref, time_ref,
     ab, trans, trig, acc, per, part, rx1, s1, rx2, full, tabuf, src, half,
-    outbuf, out_sem, int_sem, vec_sem, per_sem, ta_s, ta_r, sl_s, sl_r,
+    int_sem, vec_sem, per_sem, ta_s, ta_r, sl_s, sl_r,
     x1_s, x1_r, x2_s, x2_r, x3_s, x3_r,
 ):
     nmom = part.shape[0]
@@ -248,19 +248,17 @@
     for d in range(1, n):
         sl_copy(d).wait_recv()
     s_high, s_low = split(complex_block(src[0], src[1]))
-    stores = []
     for j in range(blocks):
         at = slice(j * rank, (j + 1) * rank)
         corr = mxu(h_high[at], s_high) + mxu(h_high[at], s_low) + mxu(h_low[at], s_high)
-        outbuf[j, 0] = corr[:, :rank]
-        outbuf[j, 1] = corr[:, rank:]
-        store = pltpu.make_async_copy(outbuf.at[j], out_ref.at[0, j], out_sem.at[j])
-        store.start()
-        stores.append(store)
-    for store in stores:
-        store.wait()
+        out_ref[0, j, 0] = corr[:, :rank]
+        out_ref[0, j, 1] = corr[:, rank:]
     for copy in sends:
         copy.wait_send()
+
+
+def in_hbm(array):
+    return pltpu.with_memory_space_constraint(array, pltpu.HBM)
 
 
 def body(vectors, peramb, momenta, sink_mom, spin_pick, src_time):
@@ -277,9 +275,9 @@
     hbm = pl.BlockSpec(memory_space=pl.ANY)
     return pl.pallas_call(
         functools.partial(kernel, n, nt, chunk, min(2048, sites)),
-        out_shape=jax.ShapeDtypeStruct((1, blocks, 2, rank, rank), F32),
+        out_shape=pltpu.VMEM((1, blocks, 2, rank, rank), F32),
         in_specs=[hbm] * 6,
-        out_specs=hbm,
+        out_specs=pl.BlockSpec(memory_space=pltpu.VMEM),
         scratch_shapes=[
             pltpu.SMEM(momenta.shape, jnp.int32),
             pltpu.SMEM(sink_mom.shape, jnp.int32),
@@ -298,8 +296,6 @@
             pltpu.VMEM((nt, 2, rows, rank), F32),
             pltpu.VMEM((2, rank, rank), F32),
             pltpu.VMEM((blocks * rank, 2 * rank), F32),
-            pltpu.VMEM((blocks, 2, rank, rank), F32),
-            dma((blocks,)),
             dma((4,)),
             dma((colours, 2)),
             dma,
@@ -310,9 +306,12 @@
             dma((nmom,)), dma((nmom,)),
         ],
         compiler_params=pltpu.CompilerParams(
-            collective_id=0, has_side_effects=True, vmem_limit_bytes=67043328
+            collective_id=0, has_side_effects=True, vmem_limit_bytes=50*2**20
         ),
-    )(momenta, sink_mom, spin_pick, src_time, vectors, peramb)
+    )(
+        in_hbm(momenta), in_hbm(sink_mom), in_hbm(spin_pick), src_time,
+        in_hbm(vectors), in_hbm(peramb),
+    )
 
 
 def solution(mesh):

time: 23.7 us -> 21.9 us (0.924)
  local copies, waits for them, and re-layouts: 1.87 us -> 0.8 us
  Pallas kernels: 21 us -> 20.3 us
    unnamed x1, local copies, waits for them, and re-layouts: 1.87 us -> 0.8 us
    pallas_call x1, Pallas kernels: 21 us -> 20.3 us  [body(): pl.pallas_call(functools.partial(kernel, n, nt, chunk, min(2048, sites)),...]
where the time goes in v1:
time: 21.9 us; the launch traced here: 21.7 us
  Pallas kernels  20.3 us (93%)
  local copies, waits for them, and re-layouts  0.8 us (4%)
  between operations  0.66 us (3%)
    pallas_call x1, Pallas kernels, body(): pl.pallas_call(functools.partial(kernel, n, nt, chunk, min(2048, sites)),...  20.3 us
    unnamed x1, local copies, waits for them, and re-layouts  0.8 us

profile of v1, /device:TPU:0, one launch (start us, length us, event | category | flops | bytes accessed | tf_op | source)
XLA Modules:
  0.0 21.7 jit_solution(2530370444095081867)
XLA Ops:
  0.7 20.3 %shard_map.64 = f32[1,4,2,128,128]{4,3,2,1,0:T(8,128)S(1)} custom-call(s32[4,3]{1,0:T(4,128)} %mom_hbm.1, s32[16]{0:T(128)} %sink_hbm.1, s32[16]{0:T(128)} %pick_hbm.1, s32[1]{0:T(128)S(6)} %copy.9.time_hbm, bf16[1,2,3,2048,128]{4,3,2,1,0:T(8,128)(2,1)} %vec_hbm.1, bf16[1,16,2,128,128]{4,3,2,1,0:T(8,128)(2,1)} %per_hbm.1), custom_call_target="tpu_custom_call" | custom-call | tf_op jit(solution)/shard_map/pallas_call | solution.py:276
  20.9 0.8 %copy.8 = f32[1,4,2,128,128]{4,3,2,1,0:T(8,128)} copy(f32[1,4,2,128,128]{4,3,2,1,0:T(8,128)S(1)} %shard_map.64) | data formatting | bytes 1048576

commit v2 on v1

--- a/solution.py
+++ b/solution.py
@@ -32,7 +32,7 @@
 
 
 def kernel(
-    n, nt, chunk, piece,
+    n, nt, chunk, turned,
     mom_hbm, sink_hbm, pick_hbm, time_hbm, vec_hbm, per_hbm,
     out_ref,
     mom_ref, sink_ref, pick_ref, time_ref,
@@ -120,21 +120,22 @@
     scale = 1.0 / math.sqrt(colours * sites * n)
 
     def accumulate(p, col):
-        @pl.loop(0, sites // chunk)
-        def _(i):
-            at = pl.ds(pl.multiple_of(i * chunk, chunk), chunk)
+        for i in range(sites // chunk):
+            at = slice(i * chunk, (i + 1) * chunk)
             a = trans[col, 0, :, at]
             b = trans[col, 1, :, at]
             c = trig[0, p : p + 1, at]
             s = trig[1, p : p + 1, at]
-            phased = jnp.concatenate(
-                [(a * c + b * s).astype(BF16), (b * c - a * s).astype(BF16)], axis=0
-            )
-            acc[...] += mxu(phased, ab[col, at, :])
+            for k, phased in enumerate((a * c + b * s, b * c - a * s)):
+                product = mxu(phased.astype(BF16), ab[col, at, :])
+                if col == 0 and i == 0:
+                    acc[k] = product
+                else:
+                    acc[k] += product
 
     def finish(p):
-        part[p, 0] = (acc[:rank, :rank] + acc[rank:, rank:]).T * scale
-        part[p, 1] = (acc[rank:, :rank] - acc[:rank, rank:]).T * scale
+        part[p, 0] = (acc[0, :, :rank] + acc[1, :, rank:]).T * scale
+        part[p, 1] = (acc[1, :, :rank] - acc[0, :, rank:]).T * scale
 
     def band(at, size):
         return pl.ds(pl.multiple_of(at * size, size), size)
@@ -198,42 +199,41 @@
                 go(ta_copy(d))
         go(x3_copy(p))
 
-    acc[...] = jnp.zeros_like(acc)
-    for col in range(colours):
+    eye = jnp.where(
+        lax.broadcasted_iota(jnp.int32, (2 * rank, 2 * rank), 0)
+        == lax.broadcasted_iota(jnp.int32, (2 * rank, 2 * rank), 1),
+        1.0, 0.0,
+    ).astype(BF16)
+    def turn(col):
         loads[2 * col].wait()
         loads[2 * col + 1].wait()
-
-        @pl.loop(0, sites // piece)
-        def _(i):
-            at = pl.ds(pl.multiple_of(i * piece, piece), piece)
-            for ri in range(2):
-                trans[col, ri, :, at] = ab[col, at, ri * rank : (ri + 1) * rank].astype(F32).T
-
+        for ri in range(2):
+            trans[col, ri, :, :turned] = ab[col, :turned, ri * rank : (ri + 1) * rank].astype(F32).T
+        if turned < sites:
+            rest = lax.dot_general(
+                eye, ab[col, turned:, :], (((1,), (1,)), ((), ())), preferred_element_type=F32
+            )
+            trans[col, 0, :, turned:] = rest[:rank]
+            trans[col, 1, :, turned:] = rest[rank:]
+
+    turn(0)
+    for col in range(colours):
+        if col + 1 < colours:
+            turn(col + 1)
         accumulate(0, col)
     finish(0)
     pl.semaphore_wait(barrier, n + nt - 2)
     go(x1_copy(0))
     for p in range(1, nmom):
-        acc[...] = jnp.zeros_like(acc)
         for col in range(colours):
             accumulate(p, col)
+        step2(p - 1)
         finish(p)
         go(x1_copy(p))
-        if p == 1:
-            step2(0)
-        if p == 3:
-            step2(1)
-    if nmom == 1:
-        step2(0)
-    step3(0)
-    for p in range(2 if nmom > 3 else 1, nmom):
-        step2(p)
-    for p in range(1, nmom):
-        if p == nmom - 1:
-            p0_select()
+    step2(nmom - 1)
+    for p in range(nmom):
         step3(p)
-    if nmom == 1:
-        p0_select()
+    p0_select()
 
     per_load.wait()
     for p in range(nmom):
@@ -270,11 +270,12 @@
     blocks = spins // n
     rows = rank // n
     chips = n // 2
-    chunk = min(2048, sites)
+    chunk = min(1024, sites)
+    turned = sites * 7 // 8 // 256 * 256
     dma = pltpu.SemaphoreType.DMA
     hbm = pl.BlockSpec(memory_space=pl.ANY)
     return pl.pallas_call(
-        functools.partial(kernel, n, nt, chunk, min(2048, sites)),
+        functools.partial(kernel, n, nt, chunk, turned),
         out_shape=pltpu.VMEM((1, blocks, 2, rank, rank), F32),
         in_specs=[hbm] * 6,
         out_specs=pl.BlockSpec(memory_space=pltpu.VMEM),
@@ -286,7 +287,7 @@
             pltpu.VMEM((colours, sites, 2 * rank), BF16),
             pltpu.VMEM((colours, 2, rank, sites), F32),
             pltpu.VMEM((2, 8, sites), F32),
-            pltpu.VMEM((2 * rank, 2 * rank), F32),
+            pltpu.VMEM((2, rank, 2 * rank), F32),
             pltpu.VMEM(peramb.shape[1:], BF16),
             pltpu.VMEM((nmom, 2, rank, rank), F32),
             pltpu.VMEM((nmom, 2, rank // 2, rank), F32),

time: 21.9 us -> 20.7 us (0.945)
  Pallas kernels: 20.3 us -> 19.1 us
    pallas_call x1, Pallas kernels: 20.3 us -> 19.1 us  [body(): pl.pallas_call(functools.partial(kernel, n, nt, chunk, turned), out_shape...]
where the time goes in v2:
time: 20.7 us; the launch traced here: 20.6 us
  Pallas kernels  19.1 us (92%)
  local copies, waits for them, and re-layouts  0.8 us (4%)
  between operations  0.66 us (3%)
    pallas_call x1, Pallas kernels, body(): pl.pallas_call(functools.partial(kernel, n, nt, chunk, turned), out_shape...  19.1 us
    unnamed x1, local copies, waits for them, and re-layouts  0.8 us

profile of v2, /device:TPU:0, one launch (start us, length us, event | category | flops | bytes accessed | tf_op | source)
XLA Modules:
  0.0 20.6 jit_solution(5464641219400881087)
XLA Ops:
  0.7 19.1 %shard_map.64 = f32[1,4,2,128,128]{4,3,2,1,0:T(8,128)S(1)} custom-call(s32[4,3]{1,0:T(4,128)} %mom_hbm.1, s32[16]{0:T(128)} %sink_hbm.1, s32[16]{0:T(128)} %pick_hbm.1, s32[1]{0:T(128)S(6)} %copy.9.time_hbm, bf16[1,2,3,2048,128]{4,3,2,1,0:T(8,128)(2,1)} %vec_hbm.1, bf16[1,16,2,128,128]{4,3,2,1,0:T(8,128)(2,1)} %per_hbm.1), custom_call_target="tpu_custom_call" | custom-call | tf_op jit(solution)/shard_map/pallas_call | solution.py:277
  19.8 0.8 %copy.8 = f32[1,4,2,128,128]{4,3,2,1,0:T(8,128)} copy(f32[1,4,2,128,128]{4,3,2,1,0:T(8,128)S(1)} %shard_map.64) | data formatting | bytes 1048576

commit v3 on v2

--- a/solution.py
+++ b/solution.py
@@ -36,8 +36,8 @@
     mom_hbm, sink_hbm, pick_hbm, time_hbm, vec_hbm, per_hbm,
     out_ref,
     mom_ref, sink_ref, pick_ref, time_ref,
-    ab, trans, trig, acc, per, part, rx1, s1, rx2, full, tabuf, src, half,
-    int_sem, vec_sem, per_sem, ta_s, ta_r, sl_s, sl_r,
+    ab, trans, trig, acc, per, part, rxq, rx1, s1, rx2, full, tabuf, src, half,
+    int_sem, vec_sem, per_sem, rs_s, rs_r, ta_s, ta_r, sl_s, sl_r,
     x1_s, x1_r, x2_s, x2_r, x3_s, x3_r,
 ):
     nmom = part.shape[0]
@@ -140,8 +140,17 @@
     def band(at, size):
         return pl.ds(pl.multiple_of(at * size, size), size)
 
-    mine = pl.ds(pl.multiple_of(core * hrows + lax.div(g, 2) * rows, rows), rows)
     sends = []
+
+    def quarter(owner):
+        at = lax.rem(owner, 2) * hrows + lax.div(owner, 2) * rows
+        return pl.ds(pl.multiple_of(at, rows), rows)
+
+    def rs_copy(d):
+        return remote(
+            part.at[0, :, quarter(ahead(d))], rxq.at[d - 1], rs_s.at[d - 1], rs_r.at[d - 1],
+            gx=ahead(d),
+        )
 
     def ta_copy(d):
         return remote(
@@ -172,6 +181,17 @@
     def go(copy):
         copy.start()
         sends.append(copy)
+
+    mine = quarter(g)
+
+    def p0_scatter():
+        total = part[0, :, mine]
+        for d in range(1, n):
+            rs_copy(d).wait_recv()
+            total = total + rxq[d - 1]
+        tabuf[t] = total
+        for d in range(1, nt):
+            go(ta_copy(d))
 
     def p0_select():
         for d in range(1, nt):
@@ -193,10 +213,6 @@
             x2_copy(p, d).wait_recv()
             total = total + rx2[p, d - 1]
         full[p, :, band(core, hrows)] = total
-        if p == 0:
-            tabuf[t] = full[0, :, mine]
-            for d in range(1, nt):
-                go(ta_copy(d))
         go(x3_copy(p))
 
     eye = jnp.where(
@@ -223,6 +239,8 @@
         accumulate(0, col)
     finish(0)
     pl.semaphore_wait(barrier, n + nt - 2)
+    for d in range(1, n):
+        go(rs_copy(d))
     go(x1_copy(0))
     for p in range(1, nmom):
         for col in range(colours):
@@ -230,10 +248,12 @@
         step2(p - 1)
         finish(p)
         go(x1_copy(p))
+    p0_scatter()
     step2(nmom - 1)
-    for p in range(nmom):
+    for p in range(nmom - 1):
         step3(p)
     p0_select()
+    step3(nmom - 1)
 
     per_load.wait()
     for p in range(nmom):
@@ -290,6 +310,7 @@
             pltpu.VMEM((2, rank, 2 * rank), F32),
             pltpu.VMEM(peramb.shape[1:], BF16),
             pltpu.VMEM((nmom, 2, rank, rank), F32),
+            pltpu.VMEM((n - 1, 2, rows, rank), F32),
             pltpu.VMEM((nmom, 2, rank // 2, rank), F32),
             pltpu.VMEM((nmom, 2, rank // 2, rank), F32),
             pltpu.VMEM((nmom, max(chips - 1, 1), 2, rank // 2, rank), F32),
@@ -300,6 +321,7 @@
             dma((4,)),
             dma((colours, 2)),
             dma,
+            dma((n - 1,)), dma((n - 1,)),
             dma((max(nt - 1, 1),)), dma((max(nt - 1, 1),)),
             dma((n - 1,)), dma((n - 1,)),
             dma((nmom,)), dma((nmom,)),

time: 20.7 us -> 19.8 us (0.957)
  Pallas kernels: 19.1 us -> 18.2 us
    pallas_call x1, Pallas kernels: 19.1 us -> 18.2 us  [body(): pl.pallas_call(functools.partial(kernel, n, nt, chunk, turned), out_shape...]
where the time goes in v3:
time: 19.8 us; the launch traced here: 19.7 us
  Pallas kernels  18.2 us (92%)
  local copies, waits for them, and re-layouts  0.8 us (4%)
  between operations  0.66 us (3%)
    pallas_call x1, Pallas kernels, body(): pl.pallas_call(functools.partial(kernel, n, nt, chunk, turned), out_shape...  18.2 us
    unnamed x1, local copies, waits for them, and re-layouts  0.8 us

profile of v3, /device:TPU:0, one launch (start us, length us, event | category | flops | bytes accessed | tf_op | source)
XLA Modules:
  0.0 19.7 jit_solution(13626786422395416247)
XLA Ops:
  0.7 18.2 %shard_map.64 = f32[1,4,2,128,128]{4,3,2,1,0:T(8,128)S(1)} custom-call(s32[4,3]{1,0:T(4,128)} %mom_hbm.1, s32[16]{0:T(128)} %sink_hbm.1, s32[16]{0:T(128)} %pick_hbm.1, s32[1]{0:T(128)S(6)} %copy.9.time_hbm, bf16[1,2,3,2048,128]{4,3,2,1,0:T(8,128)(2,1)} %vec_hbm.1, bf16[1,16,2,128,128]{4,3,2,1,0:T(8,128)(2,1)} %per_hbm.1), custom_call_target="tpu_custom_call" | custom-call | tf_op jit(solution)/shard_map/pallas_call | solution.py:297
  18.9 0.8 %copy.8 = f32[1,4,2,128,128]{4,3,2,1,0:T(8,128)} copy(f32[1,4,2,128,128]{4,3,2,1,0:T(8,128)S(1)} %shard_map.64) | data formatting | bytes 1048576

commit v4 on v3

--- a/solution.py
+++ b/solution.py
@@ -32,7 +32,7 @@
 
 
 def kernel(
-    n, nt, chunk, turned,
+    n, nt, chunk,
     mom_hbm, sink_hbm, pick_hbm, time_hbm, vec_hbm, per_hbm,
     out_ref,
     mom_ref, sink_ref, pick_ref, time_ref,
@@ -215,27 +215,11 @@
         full[p, :, band(core, hrows)] = total
         go(x3_copy(p))
 
-    eye = jnp.where(
-        lax.broadcasted_iota(jnp.int32, (2 * rank, 2 * rank), 0)
-        == lax.broadcasted_iota(jnp.int32, (2 * rank, 2 * rank), 1),
-        1.0, 0.0,
-    ).astype(BF16)
-    def turn(col):
+    for col in range(colours):
         loads[2 * col].wait()
         loads[2 * col + 1].wait()
         for ri in range(2):
-            trans[col, ri, :, :turned] = ab[col, :turned, ri * rank : (ri + 1) * rank].astype(F32).T
-        if turned < sites:
-            rest = lax.dot_general(
-                eye, ab[col, turned:, :], (((1,), (1,)), ((), ())), preferred_element_type=F32
-            )
-            trans[col, 0, :, turned:] = rest[:rank]
-            trans[col, 1, :, turned:] = rest[rank:]
-
-    turn(0)
-    for col in range(colours):
-        if col + 1 < colours:
-            turn(col + 1)
+            trans[col, ri] = ab[col, :, ri * rank : (ri + 1) * rank].T.astype(F32)
         accumulate(0, col)
     finish(0)
     pl.semaphore_wait(barrier, n + nt - 2)
@@ -291,11 +275,10 @@
     rows = rank // n
     chips = n // 2
     chunk = min(1024, sites)
-    turned = sites * 7 // 8 // 256 * 256
     dma = pltpu.SemaphoreType.DMA
     hbm = pl.BlockSpec(memory_space=pl.ANY)
     return pl.pallas_call(
-        functools.partial(kernel, n, nt, chunk, turned),
+        functools.partial(kernel, n, nt, chunk),
         out_shape=pltpu.VMEM((1, blocks, 2, rank, rank), F32),
         in_specs=[hbm] * 6,
         out_specs=pl.BlockSpec(memory_space=pltpu.VMEM),

time: 19.8 us -> 19.4 us (0.980)
  Pallas kernels: 18.2 us -> 17.8 us
    pallas_call x1, Pallas kernels: 18.2 us -> 17.8 us  [body(): pl.pallas_call(functools.partial(kernel, n, nt, chunk), out_shape=pltpu.V...]
where the time goes in v4:
time: 19.4 us; the launch traced here: 19.2 us
  Pallas kernels  17.8 us (92%)
  local copies, waits for them, and re-layouts  0.8 us (4%)
  between operations  0.66 us (3%)
    pallas_call x1, Pallas kernels, body(): pl.pallas_call(functools.partial(kernel, n, nt, chunk), out_shape=pltpu.V...  17.8 us
    unnamed x1, local copies, waits for them, and re-layouts  0.8 us

profile of v4, /device:TPU:0, one launch (start us, length us, event | category | flops | bytes accessed | tf_op | source)
XLA Modules:
  0.0 19.2 jit_solution(8584429104026344580)
XLA Ops:
  0.7 17.8 %shard_map.64 = f32[1,4,2,128,128]{4,3,2,1,0:T(8,128)S(1)} custom-call(s32[4,3]{1,0:T(4,128)} %mom_hbm.1, s32[16]{0:T(128)} %sink_hbm.1, s32[16]{0:T(128)} %pick_hbm.1, s32[1]{0:T(128)S(6)} %copy.9.time_hbm, bf16[1,2,3,2048,128]{4,3,2,1,0:T(8,128)(2,1)} %vec_hbm.1, bf16[1,16,2,128,128]{4,3,2,1,0:T(8,128)(2,1)} %per_hbm.1), custom_call_target="tpu_custom_call" | custom-call | tf_op jit(solution)/shard_map/pallas_call | solution.py:280
  18.4 0.8 %copy.8 = f32[1,4,2,128,128]{4,3,2,1,0:T(8,128)} copy(f32[1,4,2,128,128]{4,3,2,1,0:T(8,128)S(1)} %shard_map.64) | data formatting | bytes 1048576

commit v5 on v4

--- a/solution.py
+++ b/solution.py
@@ -34,7 +34,7 @@
 def kernel(
     n, nt, chunk,
     mom_hbm, sink_hbm, pick_hbm, time_hbm, vec_hbm, per_hbm,
-    out_ref,
+    h_out, s_out,
     mom_ref, sink_ref, pick_ref, time_ref,
     ab, trans, trig, acc, per, part, rxq, rx1, s1, rx2, full, tabuf, src, half,
     int_sem, vec_sem, per_sem, rs_s, rs_r, ta_s, ta_r, sl_s, sl_r,
@@ -43,7 +43,7 @@
     nmom = part.shape[0]
     rank = part.shape[-1]
     colours, sites = ab.shape[0], ab.shape[1]
-    blocks = out_ref.shape[1]
+    blocks = h_out.shape[1] // rank
     rows = rank // n
     hrows = rank // 2
     g = lax.axis_index("gx")
@@ -77,13 +77,15 @@
             barrier, inc=1, device_id={"ta": lax.rem(t + d, nt)}, device_id_type=MESH
         )
 
+    lead = sites // 2
+    pieces = [(0, 0, lead), (0, lead, sites)] + [(col, 0, sites) for col in range(1, colours)]
     loads = []
-    for col in range(colours):
+    for i, (col, lo, hi) in enumerate(pieces):
         for ri in range(2):
             load = pltpu.make_async_copy(
-                vec_hbm.at[0, ri, col],
-                ab.at[col, :, pl.ds(ri * rank, rank)],
-                vec_sem.at[col, ri],
+                vec_hbm.at[0, ri, col, lo:hi],
+                ab.at[col, lo:hi, ri * rank : (ri + 1) * rank],
+                vec_sem.at[i, ri],
             )
             load.start()
             loads.append(load)
@@ -119,9 +121,9 @@
 
     scale = 1.0 / math.sqrt(colours * sites * n)
 
-    def accumulate(p, col):
-        for i in range(sites // chunk):
-            at = slice(i * chunk, (i + 1) * chunk)
+    def accumulate(p, col, lo, hi):
+        for i in range(lo, hi, chunk):
+            at = slice(i, i + chunk)
             a = trans[col, 0, :, at]
             b = trans[col, 1, :, at]
             c = trig[0, p : p + 1, at]
@@ -146,6 +148,8 @@
         at = lax.rem(owner, 2) * hrows + lax.div(owner, 2) * rows
         return pl.ds(pl.multiple_of(at, rows), rows)
 
+    mine = quarter(g)
+
     def rs_copy(d):
         return remote(
             part.at[0, :, quarter(ahead(d))], rxq.at[d - 1], rs_s.at[d - 1], rs_r.at[d - 1],
@@ -172,6 +176,12 @@
         return remote(
             s1.at[p], rx2.at[p, d - 1], x2_s.at[p, d - 1], x2_r.at[p, d - 1],
             gx=ahead(2 * d),
+        )
+
+    def sink_copy(d):
+        rows_out = full.at[0, :, mine]
+        return remote(
+            rows_out, rows_out, x2_s.at[0, d - 1], x2_r.at[0, d - 1], gx=ahead(2 * d)
         )
 
     def x3_copy(p):
@@ -181,8 +191,6 @@
     def go(copy):
         copy.start()
         sends.append(copy)
-
-    mine = quarter(g)
 
     def p0_scatter():
         total = part[0, :, mine]
@@ -192,6 +200,9 @@
         tabuf[t] = total
         for d in range(1, nt):
             go(ta_copy(d))
+        full[0, :, mine] = total
+        for d in range(1, chips):
+            go(sink_copy(d))
 
     def p0_select():
         for d in range(1, nt):
@@ -207,6 +218,11 @@
         for d in range(1, chips):
             go(x2_copy(p, d))
 
+    def p0_sink():
+        for d in range(1, chips):
+            sink_copy(d).wait_recv()
+        go(x3_copy(0))
+
     def step3(p):
         total = s1[p]
         for d in range(1, chips):
@@ -215,29 +231,37 @@
         full[p, :, band(core, hrows)] = total
         go(x3_copy(p))
 
-    for col in range(colours):
-        loads[2 * col].wait()
-        loads[2 * col + 1].wait()
+    for i, (col, lo, hi) in enumerate(pieces):
+        loads[2 * i].wait()
+        loads[2 * i + 1].wait()
         for ri in range(2):
-            trans[col, ri] = ab[col, :, ri * rank : (ri + 1) * rank].T.astype(F32)
-        accumulate(0, col)
+            trans[col, ri, :, lo:hi] = ab[col, lo:hi, ri * rank : (ri + 1) * rank].T.astype(F32)
+        accumulate(0, col, lo, hi)
     finish(0)
     pl.semaphore_wait(barrier, n + nt - 2)
     for d in range(1, n):
         go(rs_copy(d))
-    go(x1_copy(0))
     for p in range(1, nmom):
         for col in range(colours):
-            accumulate(p, col)
-        step2(p - 1)
+            accumulate(p, col, 0, sites)
+            if p > 2 and col == 0:
+                step2(p - 2)
+        if p == nmom - 1:
+            p0_scatter()
+            if p > 1:
+                step2(p - 1)
         finish(p)
         go(x1_copy(p))
-    p0_scatter()
-    step2(nmom - 1)
-    for p in range(nmom - 1):
+    if nmom > 1:
+        step2(nmom - 1)
+    else:
+        p0_scatter()
+    for p in range(1, nmom - 1):
         step3(p)
+    p0_sink()
     p0_select()
-    step3(nmom - 1)
+    if nmom > 1:
+        step3(nmom - 1)
 
     per_load.wait()
     for p in range(nmom):
@@ -248,17 +272,30 @@
         e_high, e_low = split(jnp.concatenate([full[sink, 0], full[sink, 1]], axis=1))
         spin = complex_block(per[pick, 0], per[pick, 1])
         half[j * rank : (j + 1) * rank] = mxu(e_high, spin) + mxu(e_low, spin)
-    h_high, h_low = split(half[...] * (1.0 / math.sqrt(rank)))
+    h_out[0], h_out[1] = split(half[...] * (1.0 / math.sqrt(rank)))
     for d in range(1, n):
         sl_copy(d).wait_recv()
-    s_high, s_low = split(complex_block(src[0], src[1]))
+    s_out[0], s_out[1] = split(complex_block(src[0], src[1]))
+    for copy in sends:
+        copy.wait_send()
+
+
+def close(h_ref, s_ref, out_hbm, outbuf, sems):
+    blocks = outbuf.shape[0]
+    rank = outbuf.shape[-1]
+    stores = []
     for j in range(blocks):
         at = slice(j * rank, (j + 1) * rank)
-        corr = mxu(h_high[at], s_high) + mxu(h_high[at], s_low) + mxu(h_low[at], s_high)
-        out_ref[0, j, 0] = corr[:, :rank]
-        out_ref[0, j, 1] = corr[:, rank:]
-    for copy in sends:
-        copy.wait_send()
+        corr = (
+            mxu(h_ref[0, at], s_ref[0]) + mxu(h_ref[0, at], s_ref[1]) + mxu(h_ref[1, at], s_ref[0])
+        )
+        outbuf[j, 0] = corr[:, :rank]
+        outbuf[j, 1] = corr[:, rank:]
+        store = pltpu.make_async_copy(outbuf.at[j], out_hbm.at[0, j], sems.at[j])
+        store.start()
+        stores.append(store)
+    for store in stores:
+        store.wait()
 
 
 def in_hbm(array):
@@ -274,14 +311,17 @@
     blocks = spins // n
     rows = rank // n
     chips = n // 2
-    chunk = min(1024, sites)
+    chunk = min(1024, sites // 2)
     dma = pltpu.SemaphoreType.DMA
     hbm = pl.BlockSpec(memory_space=pl.ANY)
-    return pl.pallas_call(
+    h, s = pl.pallas_call(
         functools.partial(kernel, n, nt, chunk),
-        out_shape=pltpu.VMEM((1, blocks, 2, rank, rank), F32),
+        out_shape=(
+            pltpu.VMEM((2, blocks * rank, 2 * rank), BF16),
+            pltpu.VMEM((2, 2 * rank, 2 * rank), BF16),
+        ),
         in_specs=[hbm] * 6,
-        out_specs=pl.BlockSpec(memory_space=pltpu.VMEM),
+        out_specs=(pl.BlockSpec(memory_space=pltpu.VMEM),) * 2,
         scratch_shapes=[
             pltpu.SMEM(momenta.shape, jnp.int32),
             pltpu.SMEM(sink_mom.shape, jnp.int32),
@@ -302,7 +342,7 @@
             pltpu.VMEM((2, rank, rank), F32),
             pltpu.VMEM((blocks * rank, 2 * rank), F32),
             dma((4,)),
-            dma((colours, 2)),
+            dma((colours + 1, 2)),
             dma,
             dma((n - 1,)), dma((n - 1,)),
             dma((max(nt - 1, 1),)), dma((max(nt - 1, 1),)),
@@ -318,6 +358,14 @@
         in_hbm(momenta), in_hbm(sink_mom), in_hbm(spin_pick), src_time,
         in_hbm(vectors), in_hbm(peramb),
     )
+    return pl.pallas_call(
+        close,
+        out_shape=jax.ShapeDtypeStruct((1, blocks, 2, rank, rank), F32),
+        in_specs=[pl.BlockSpec(memory_space=pltpu.VMEM)] * 2,
+        out_specs=hbm,
+        scratch_shapes=[pltpu.VMEM((blocks, 2, rank, rank), F32), dma((blocks,))],
+        compiler_params=pltpu.CompilerParams(vmem_limit_bytes=8 * 2**20),
+    )(h, s)
 
 
 def solution(mesh):

time: 19.4 us -> 19 us (0.979)
  local copies, waits for them, and re-layouts: 0.8 us -> 0 us
  Pallas kernels: 17.8 us -> 18.1 us
    unnamed x1 -> x0, local copies, waits for them, and re-layouts: 0.8 us -> none
    pallas_call x1 -> x2, Pallas kernels: 17.8 us -> 18.1 us  [the longest x1 17 us: body(): pl.pallas_call(functools.partial(kernel, n, nt, chunk), out_shape=(pltpu....]
where the time goes in v5:
time: 19 us; the launch traced here: 18.8 us
  Pallas kernels  18.1 us (95%)
  between operations  0.66 us (3%)
    pallas_call x1, Pallas kernels, body(): pl.pallas_call(functools.partial(kernel, n, nt, chunk), out_shape=(pltpu....  17 us
    pallas_call x1, Pallas kernels, body(): pl.pallas_call(close, out_shape=jax.ShapeDtypeStruct((1, blocks, 2, rank,...  1.12 us

profile of v5, /device:TPU:0, one launch (start us, length us, event | category | flops | bytes accessed | tf_op | source)
XLA Modules:
  0.0 18.8 jit_solution(17777775668694185578)
XLA Ops:
  0.7 17.0 %shard_map.64 = (bf16[2,512,256]{2,1,0:T(8,128)(2,1)S(1)}, bf16[2,256,256]{2,1,0:T(8,128)(2,1)S(1)}) custom-call(s32[4,3]{1,0:T(4,128)} %mom_hbm.1, s32[16]{0:T(128)} %sink_hbm.1, s32[16]{0:T(128)} %pick_hbm.1, s32[1]{0:T(128)S(6)} %copy.7.time_hbm, bf16[1,2,3,2048,128]{4,3,2,1,0:T(8,128)(2,1)} %vec_hbm.1, bf16[1,16,2,128,128]{4,3,2,1,0:T(8,128)(2,1)} %per_hbm.1), custom_call_target="tpu_custom_call" | custom-call | tf_op jit(solution)/shard_map/pallas_call | solution.py:317
  17.7 1.1 %shard_map.65 = f32[1,4,2,128,128]{4,3,2,1,0:T(8,128)} custom-call(bf16[2,512,256]{2,1,0:T(8,128)(2,1)S(1)} %get-tuple-element.7.h_ref, bf16[2,256,256]{2,1,0:T(8,128)(2,1)S(1)} %get-tuple-element.8.s_ref), custom_call_target="tpu_custom_call" | custom-call | tf_op jit(solution)/shard_map/pallas_call | solution.py:361

commit v6 on v5

--- a/solution.py
+++ b/solution.py
@@ -51,9 +51,15 @@
     core = lax.rem(g, 2)
     partner = g + 1 - 2 * core
     chips = n // 2
+    chip = lax.div(g, 2)
+    own = lax.rem(core + chip, 2)
 
     def ahead(d):
         return lax.rem(g + d, n)
+
+    def across(d):
+        other = lax.rem(chip + d, chips)
+        return 2 * other + lax.rem(own + other, 2)
 
     def remote(src_ref, dst_ref, ss, rs, **where):
         return pltpu.make_async_remote_copy(
@@ -145,10 +151,12 @@
     sends = []
 
     def quarter(owner):
-        at = lax.rem(owner, 2) * hrows + lax.div(owner, 2) * rows
+        part_of = lax.rem(lax.rem(owner, 2) + lax.div(owner, 2), 2)
+        at = part_of * hrows + lax.div(owner, 2) * rows
         return pl.ds(pl.multiple_of(at, rows), rows)
 
     mine = quarter(g)
+    order = sorted(range(1, n), key=lambda d: d % 2)
 
     def rs_copy(d):
         return remote(
@@ -168,24 +176,24 @@
 
     def x1_copy(p):
         return remote(
-            part.at[p, :, band(1 - core, hrows)], rx1.at[p], x1_s.at[p], x1_r.at[p],
+            part.at[p, :, band(1 - own, hrows)], rx1.at[p], x1_s.at[p], x1_r.at[p],
             gx=partner,
         )
 
     def x2_copy(p, d):
         return remote(
             s1.at[p], rx2.at[p, d - 1], x2_s.at[p, d - 1], x2_r.at[p, d - 1],
-            gx=ahead(2 * d),
+            gx=across(d),
         )
 
     def sink_copy(d):
         rows_out = full.at[0, :, mine]
         return remote(
-            rows_out, rows_out, x2_s.at[0, d - 1], x2_r.at[0, d - 1], gx=ahead(2 * d)
+            rows_out, rows_out, x2_s.at[0, d - 1], x2_r.at[0, d - 1], gx=across(d)
         )
 
     def x3_copy(p):
-        keep = full.at[p, :, band(core, hrows)]
+        keep = full.at[p, :, band(own, hrows)]
         return remote(keep, keep, x3_s.at[p], x3_r.at[p], gx=partner)
 
     def go(copy):
@@ -209,12 +217,12 @@
             ta_copy(d).wait_recv()
         root = lax.rem(time_ref[0], nt)
         src[:, mine] = tabuf[root]
-        for d in range(1, n):
+        for d in order:
             go(sl_copy(d))
 
     def step2(p):
         x1_copy(p).wait_recv()
-        s1[p] = part[p, :, band(core, hrows)] + rx1[p]
+        s1[p] = part[p, :, band(own, hrows)] + rx1[p]
         for d in range(1, chips):
             go(x2_copy(p, d))
 
@@ -228,7 +236,7 @@
         for d in range(1, chips):
             x2_copy(p, d).wait_recv()
             total = total + rx2[p, d - 1]
-        full[p, :, band(core, hrows)] = total
+        full[p, :, band(own, hrows)] = total
         go(x3_copy(p))
 
     for i, (col, lo, hi) in enumerate(pieces):
@@ -239,7 +247,7 @@
         accumulate(0, col, lo, hi)
     finish(0)
     pl.semaphore_wait(barrier, n + nt - 2)
-    for d in range(1, n):
+    for d in order:
         go(rs_copy(d))
     for p in range(1, nmom):
         for col in range(colours):

time: 19 us -> 19 us (level)
  no operation moved by 1% of the time
where the time goes in v6:
time: 19 us; the launch traced here: 18.8 us
  Pallas kernels  18.2 us (96%)
  between operations  0.66 us (3%)
    pallas_call x1, Pallas kernels, body(): pl.pallas_call(functools.partial(kernel, n, nt, chunk), out_shape=(pltpu....  17 us
    pallas_call x1, Pallas kernels, body(): pl.pallas_call(close, out_shape=jax.ShapeDtypeStruct((1, blocks, 2, rank,...  1.11 us

profile of v6, /device:TPU:0, one launch (start us, length us, event | category | flops | bytes accessed | tf_op | source)
XLA Modules:
  0.0 18.8 jit_solution(16011145001208026332)
XLA Ops:
  0.7 17.0 %shard_map.64 = (bf16[2,512,256]{2,1,0:T(8,128)(2,1)S(1)}, bf16[2,256,256]{2,1,0:T(8,128)(2,1)S(1)}) custom-call(s32[4,3]{1,0:T(4,128)} %mom_hbm.1, s32[16]{0:T(128)} %sink_hbm.1, s32[16]{0:T(128)} %pick_hbm.1, s32[1]{0:T(128)S(6)} %copy.7.time_hbm, bf16[1,2,3,2048,128]{4,3,2,1,0:T(8,128)(2,1)} %vec_hbm.1, bf16[1,16,2,128,128]{4,3,2,1,0:T(8,128)(2,1)} %per_hbm.1), custom_call_target="tpu_custom_call" | custom-call | tf_op jit(solution)/shard_map/pallas_call | solution.py:325
  17.7 1.1 %shard_map.65 = f32[1,4,2,128,128]{4,3,2,1,0:T(8,128)} custom-call(bf16[2,512,256]{2,1,0:T(8,128)(2,1)S(1)} %get-tuple-element.7.h_ref, bf16[2,256,256]{2,1,0:T(8,128)(2,1)S(1)} %get-tuple-element.8.s_ref), custom_call_target="tpu_custom_call" | custom-call | tf_op jit(solution)/shard_map/pallas_call | solution.py:369

commit v7 on v5

--- a/solution.py
+++ b/solution.py
@@ -149,6 +149,7 @@
         return pl.ds(pl.multiple_of(at, rows), rows)
 
     mine = quarter(g)
+    order = sorted(range(1, n), key=lambda d: d % 2)
 
     def rs_copy(d):
         return remote(
@@ -209,7 +210,7 @@
             ta_copy(d).wait_recv()
         root = lax.rem(time_ref[0], nt)
         src[:, mine] = tabuf[root]
-        for d in range(1, n):
+        for d in order:
             go(sl_copy(d))
 
     def step2(p):
@@ -239,7 +240,7 @@
         accumulate(0, col, lo, hi)
     finish(0)
     pl.semaphore_wait(barrier, n + nt - 2)
-    for d in range(1, n):
+    for d in order:
         go(rs_copy(d))
     for p in range(1, nmom):
         for col in range(colours):

time: 19 us -> 18.9 us (level)
  no operation moved by 1% of the time
where the time goes in v7:
time: 18.9 us; the launch traced here: 18.8 us
  Pallas kernels  18.1 us (96%)
  between operations  0.66 us (3%)
    pallas_call x1, Pallas kernels, body(): pl.pallas_call(functools.partial(kernel, n, nt, chunk), out_shape=(pltpu....  17 us
    pallas_call x1, Pallas kernels, body(): pl.pallas_call(close, out_shape=jax.ShapeDtypeStruct((1, blocks, 2, rank,...  1.11 us

profile of v7, /device:TPU:0, one launch (start us, length us, event | category | flops | bytes accessed | tf_op | source)
XLA Modules:
  0.0 18.8 jit_solution(8703059245831442754)
XLA Ops:
  0.7 17.0 %shard_map.64 = (bf16[2,512,256]{2,1,0:T(8,128)(2,1)S(1)}, bf16[2,256,256]{2,1,0:T(8,128)(2,1)S(1)}) custom-call(s32[4,3]{1,0:T(4,128)} %mom_hbm.1, s32[16]{0:T(128)} %sink_hbm.1, s32[16]{0:T(128)} %pick_hbm.1, s32[1]{0:T(128)S(6)} %copy.7.time_hbm, bf16[1,2,3,2048,128]{4,3,2,1,0:T(8,128)(2,1)} %vec_hbm.1, bf16[1,16,2,128,128]{4,3,2,1,0:T(8,128)(2,1)} %per_hbm.1), custom_call_target="tpu_custom_call" | custom-call | tf_op jit(solution)/shard_map/pallas_call | solution.py:318
  17.7 1.1 %shard_map.65 = f32[1,4,2,128,128]{4,3,2,1,0:T(8,128)} custom-call(bf16[2,512,256]{2,1,0:T(8,128)(2,1)S(1)} %get-tuple-element.7.h_ref, bf16[2,256,256]{2,1,0:T(8,128)(2,1)S(1)} %get-tuple-element.8.s_ref), custom_call_target="tpu_custom_call" | custom-call | tf_op jit(solution)/shard_map/pallas_call | solution.py:362
